TPU v7x, 128 devices: a whole 4x4x4 slice. The times are simulated.
128 devices in a mesh: keys: 32 (over y, z, core), heads: 4 (over x).
Axes of the slice: x: 4, y: 4, z: 4, core: 2. Of those that a mesh axis runs over, the one named last changes fastest.
Arguments:
- main_query: bfloat16 [512, 128, 576], P(None, 'heads'), may hold values from -60 to 60
- latent_keys: bfloat16 [16384, 576], P('keys'), may hold values from -5 to 5
- index_query: bfloat16 [512, 64, 128], P(None, 'heads'), may hold values from -60 to 60
- index_keys: bfloat16 [16384, 128], P('keys'), may hold values from -5 to 5
- index_weights: float32 [512, 64], P(None, 'heads'), may hold values from -10 to 10
- query_limit: int32 [512], replicated, may hold values from 1 to 16383, as said below
Outputs:
- grad_index_query: float32 [512, 64, 128], P('keys', 'heads')
- grad_index_weights: float32 [512, 64], P('keys', 'heads')
- grad_index_keys: float32 [16384, 128], P('keys')
Inputs may be any that keep to these rules, and one draw needn't show every extreme that they name: `query_limit`: Non-decreasing over the rows; the first row's value is 1 and the last row's is 16383.
All inputs are finite; a program needn't handle non-finite values.
Results may differ from a plain program's by a relative error of at most 0.0025.
Values sent between devices are 32-bit elements; how exact they have to be, the bound alone decides.
A program may use at most 192 MiB of HBM per device.

v0:
```python
import jax
import jax.numpy as jnp
from jax import lax
from jax.sharding import PartitionSpec as P

H = 128
DL = 576
HI = 64
DI = 128


def logit_gradient(target, logits, visible, limits):
    logits = jnp.where(visible, logits, -1e30)
    logit_local = jnp.max(logits, axis=1)
    logit_max = lax.pmax(logit_local, "keys")
    local_expsum = jnp.sum(jnp.where(visible, jnp.exp(logits - logit_max[:, None]), 0.0), axis=1)
    logit_total = lax.psum(local_expsum, "keys")
    index_probs = jnp.where(
        visible, jnp.exp(logits - logit_max[:, None]) / logit_total[:, None], 0.0
    )
    return (index_probs - target) * (limits + 1).astype(jnp.float32)[:, None]


def per_device(main_query, latent_keys, index_query, index_keys, index_weights, query_limit):
    key_rows = latent_keys.shape[0]
    key_start = lax.axis_index("keys") * key_rows
    positions = key_start + lax.iota(jnp.int32, key_rows)
    visible = positions[None, :] <= query_limit[:, None]
    score_scale = 2.0 * DL ** (-0.5)
    index_scale = DI ** (-0.5)
    head_scale = HI ** (-0.5)
    scores = (
        jnp.einsum("thd,sd->hts", main_query, latent_keys, preferred_element_type=jnp.float32)
        * score_scale
    )
    scores = jnp.where(visible[None], scores, -1e30)
    local_max = jnp.max(scores, axis=2)
    row_max = lax.pmax(local_max, "keys")
    local_total = jnp.sum(
        jnp.where(visible[None], jnp.exp(scores - row_max[:, :, None]), 0.0), axis=2
    )
    row_total = lax.psum(local_total, "keys")
    head_probs = jnp.where(
        visible[None], jnp.exp(scores - row_max[:, :, None]) / row_total[:, :, None], 0.0
    )
    target_part = jnp.sum(head_probs, axis=0) / H
    index_dots = (
        jnp.einsum("tjd,sd->jts", index_query, index_keys, preferred_element_type=jnp.float32)
        * index_scale
    )
    rectified = jnp.maximum(index_dots, 0.0)
    logit_part = jnp.sum(index_weights.T[:, :, None] * rectified, axis=0) * head_scale
    target, logits = lax.psum((target_part, logit_part), "heads")
    logit_grad = logit_gradient(target, logits, visible, query_limit)
    spread = logit_grad[None] * index_weights.T[:, :, None] * head_scale
    grad_tile = jnp.where(index_dots > 0, spread, 0.0).astype(jnp.bfloat16)
    key_part = jnp.einsum("jts,tjd->sd", grad_tile, index_query, preferred_element_type=jnp.float32)
    grad_index_keys = lax.psum(key_part, "heads") * index_scale
    query_part = jnp.einsum(
        "jts,sd->tjd", grad_tile, index_keys, preferred_element_type=jnp.float32
    )
    weight_part = jnp.sum(logit_grad[None] * rectified, axis=2).T
    query_sum, weight_sum = (
        lax.psum_scatter(query_part, "keys", scatter_dimension=0, tiled=True),
        lax.psum_scatter(weight_part, "keys", scatter_dimension=0, tiled=True),
    )
    grad_index_query = query_sum * index_scale
    grad_index_weights = weight_sum * head_scale
    return (grad_index_query, grad_index_weights, grad_index_keys)


def solution(mesh):
    in_specs = (
        P(None, "heads", None),
        P("keys", None),
        P(None, "heads", None),
        P("keys", None),
        P(None, "heads"),
        P(),
    )
    out_specs = (P("keys", "heads", None), P("keys", "heads"), P("keys", None))
    return jax.shard_map(
        per_device, mesh=mesh, in_specs=in_specs, out_specs=out_specs, check_vma=False
    )
```

profile of v0, /device:TPU:24, one launch (start us, length us, event | category | flops | bytes accessed | tf_op | source)
XLA Modules:
  0.0 673.3 jit_solution(14358344279086101432)
XLA Ops:
  7.2 0.0 copy-start
  7.2 0.0 all-reduce.6.cloned.1.call-start
  7.2 1.0 broadcast_compare_fusion
  8.3 0.0 copy-start.2
  8.3 25.7 %fusion = (f32[32,512]{1,0:T(8,128)}, f32[512,512,32]{1,0,2:T(8,128)}) fusion(pred[512,512]{0,1:T(8,128)(4,1)S(1)} %broadcast_compare_fusion, bf16[512,32,576]{0,2,1:T(8,128)(2,1)} %param.6, bf16[512,576]{0,1:T(8,128)(2,1)} %param.7), kind=kOutput, calls=%fused_computation.4 | convolution fusion | flops 9688825856 | bytes 53346304 | tf_op jit(solution)/shard_map/thd,sd->hts/dot_general | solution.py:33
  34.0 0.0 all-reduce.6.cloned.1.call-update
  34.0 0.0 all-reduce.8.cloned.1.call-start
  34.0 0.0 copy-done
  34.1 0.0 copy-done.2
  34.1 8.2 %fusion.1 = (f32[512,512]{0,1:T(8,128)S(1)}, f32[512,512,16]{1,0,2:T(8,128)}) fusion(f32[16,512]{1,0:T(8,128)} %bitcast.40, bf16[512,16,128]{2,1,0:T(8,128)(2,1)S(1)} %copy-done, bf16[512,128]{1,0:T(8,128)(2,1)S(1)} %copy-done.2), kind=kOutput, calls=%fused_computation.7 | convolution fusion | flops 1090256896 | bytes 20086784 | tf_op jit(solution)/shard_map/tjd,sd->jts/dot_general | solution.py:48
  42.3 89.9 %all-reduce.6.cloned.1.call-done = f32[32,512]{1,0:T(8,128)} async-done(((f32[32,512]{1,0:T(8,128)}), f32[32,512]{1,0:T(8,128)}) %all-reduce.6.cloned.1.call-update) | async-done | bytes 65552 | tf_op jit(solution)/shard_map/pmax | solution.py:38
  132.2 15.7 %select_reduce_fusion.1 = f32[32,512]{1,0:T(8,128)} fusion(f32[512,512,32]{1,0,2:T(8,128)} %get-tuple-element.15, f32[32,512]{1,0:T(8,128)} %all-reduce.6.cloned.1.call-done, pred[512,512]{0,1:T(8,128)(4,1)S(1)} %broadcast_compare_fusion), kind=kLoop, calls=%fused_computation.2 | loop fusion | flops 41926656 | bytes 33947648 | tf_op jit(solution)/shard_map/reduce_sum | solution.py:39
  147.8 0.0 all-reduce.8.cloned.1.call-update
  147.8 0.2 all-reduce.12.cloned.1.call-start
  148.1 1.1 broadcast_multiply_fusion.1
  149.2 94.7 %all-reduce.8.cloned.1.call-done = f32[32,512]{1,0:T(8,128)} async-done(((f32[32,512]{1,0:T(8,128)}), f32[32,512]{1,0:T(8,128)}) %all-reduce.8.cloned.1.call-update) | async-done | bytes 65552 | tf_op jit(solution)/shard_map/psum | solution.py:42
  243.9 0.0 copy-done.1
  243.9 15.5 %select_reduce_fusion = f32[512,512]{0,1:T(8,128)S(1)} fusion(f32[512,512,32]{1,0,2:T(8,128)} %get-tuple-element.15, f32[32,512]{1,0:T(8,128)} %all-reduce.8.cloned.1.call-done, f32[32,512]{1,0:T(8,128)S(1)} %copy-done.1, pred[512,512]{0,1:T(8,128)(4,1)S(1)} %broadcast_compare_fusion), kind=kLoop, calls=%fused_computation.1 | loop fusion | flops 50069504 | bytes 34996224 | tf_op jit(solution)/shard_map/reduce_sum | solution.py:46
  259.4 0.0 copy-start.5
  259.4 1.1 broadcast_multiply_fusion
  260.5 0.0 all-reduce.12.cloned.1.call-update
  260.5 0.0 reduce-scatter.7.cloned.1.call-start
  260.6 0.0 copy-done.4
  260.6 58.7 %all-reduce.12.cloned.1.call-done = (f32[512,512]{0,1:T(8,128)}, f32[512,512]{0,1:T(8,128)}) async-done(((f32[512,512]{0,1:T(8,128)}, f32[512,512]{0,1:T(8,128)}), (f32[512,512]{0,1:T(8,128)}, f32[512,512]{0,1:T(8,128)})) %all-reduce.12.cloned.1.call-update) | async-done | bytes 2097168 | tf_op jit(solution)/shard_map/psum | solution.py:53
  319.3 1.4 fusion.10
  320.7 55.5 %pmax.14 = f32[512]{0:T(512)S(1)} all-reduce(f32[512]{0:T(512)S(1)} %fusion.10), channel_id=1, replica_groups=mesh['keys'=32,'heads'=4] {'keys'}, use_global_device_ids=true, to_apply=%region_3.4 | all-reduce | flops 512 | bytes 4096 | tf_op jit(solution)/shard_map/pmax | solution.py:15
  376.2 1.5 select_reduce_fusion.2
  377.8 56.4 %psum.36 = f32[512]{0:T(512)S(1)} all-reduce(f32[512]{0:T(512)S(1)} %select_reduce_fusion.2), channel_id=1, replica_groups=mesh['keys'=32,'heads'=4] {'keys'}, use_global_device_ids=true, to_apply=%region_5.6 | all-reduce | flops 512 | bytes 4096 | tf_op jit(solution)/shard_map/psum | solution.py:17
  434.1 1.9 subtract_multiply_fusion
  436.0 8.1 %fusion.2 = f32[16,512]{1,0:T(8,128)S(1)} fusion(f32[512,512,16]{1,0,2:T(8,128)} %get-tuple-element.17, f32[512,512]{0,1:T(8,128)S(1)} %subtract_multiply_fusion), kind=kLoop, calls=%fused_computation.8 | loop fusion | flops 16769024 | bytes 17858560 | tf_op jit(solution)/shard_map/reduce_sum | solution.py:62
  444.2 0.8 copy.24
  445.0 0.0 reduce-scatter.7.cloned.1.call-update
  445.0 0.0 copy-start.3
  445.0 0.0 all-reduce.10.cloned.1.call-start
  445.1 8.3 %fusion.7 = f32[512,128]{1,0:T(8,128)} fusion(bf16[512,16,128]{2,1,0:T(8,128)(2,1)S(1)} %copy-done, f32[512,512,16]{1,0,2:T(8,128)} %get-tuple-element.17, f32[512,512]{0,1:T(8,128)S(1)} %subtract_multiply_fusion, f32[16,512]{1,0:T(8,128)S(1)} %bitcast.41), kind=kOutput, calls=%fused_computation.15 | convolution fusion | flops 1098907648 | bytes 20217856 | tf_op jit(solution)/shard_map/jts,tjd->sd/dot_general | solution.py:57
  453.4 0.0 all-reduce.10.cloned.1.call-update
  453.4 0.0 reduce-scatter.5.cloned.1.call-start
  453.5 0.0 copy-done.3
  453.5 12.3 %convolution_bitcast_fusion = f32[512,16,128]{2,0,1:T(8,128)} fusion(bf16[512,128]{1,0:T(8,128)(2,1)S(1)} %copy-done.3, f32[512,512,16]{1,0,2:T(8,128)} %get-tuple-element.17, f32[512,512]{0,1:T(8,128)S(1)} %subtract_multiply_fusion, f32[16,512]{1,0:T(8,128)S(1)} %bitcast.42), kind=kOutput, calls=%fused_computation.10 | convolution fusion | flops 1098907648 | bytes 22183936 | tf_op jit(solution)/shard_map/jts,sd->tjd/dot_general | solution.py:59
  465.8 0.0 reduce-scatter.5.cloned.1.call-update
  465.8 69.2 %reduce-scatter.7.cloned.1.call-done = f32[16,16]{1,0:T(8,128)} async-done(((f32[512,16]{1,0:T(8,128)}), f32[16,16]{1,0:T(8,128)}) %reduce-scatter.7.cloned.1.call-update) | async-done | bytes 1040
  535.0 0.8 copy.25
  535.8 0.7 copy.22
  536.5 42.2 %all-reduce.10.cloned.1.call-done = f32[512,128]{1,0:T(8,128)} async-done(((f32[512,128]{1,0:T(8,128)}), f32[512,128]{1,0:T(8,128)}) %all-reduce.10.cloned.1.call-update) | async-done | bytes 262160 | tf_op jit(solution)/shard_map/psum | solution.py:58
  578.6 1.7 broadcast_multiply_fusion.2
  580.3 84.5 %reduce-scatter.5.cloned.1.call-done = f32[16,16,128]{2,0,1:T(8,128)} async-done(((f32[512,16,128]{2,0,1:T(8,128)}), f32[16,16,128]{2,0,1:T(8,128)}) %reduce-scatter.5.cloned.1.call-update) | async-done | bytes 131088 | tf_op jit(solution)/shard_map/reduce_scatter | solution.py:64
  664.9 0.9 broadcast_multiply_fusion.3
  665.8 0.7 copy.21
  (6 shorter events, 0.0 us)
Async XLA Ops:
  7.2 26.9 %copy-start = (bf16[512,16,128]{2,1,0:T(8,128)(2,1)S(1)}, bf16[512,16,128]{2,1,0:T(8,128)(2,1)}, u32[]{:S(2)}) copy-start(bf16[512,16,128]{2,1,0:T(8,128)(2,1)} %param.8) | copy-start | bytes 6291460
  7.2 125.0 %all-reduce.6.cloned.1.call-start = ((), (), s32[]{:S(2)}) async-start(), calls=%async_computation.2 | async-start | bytes 131072 | tf_op jit(solution)/shard_map/pmax | solution.py:38
  8.3 25.8 %copy-start.2 = (bf16[512,128]{1,0:T(8,128)(2,1)S(1)}, bf16[512,128]{1,0:T(8,128)(2,1)}, u32[]{:S(2)}) copy-start(bf16[512,128]{1,0:T(8,128)(2,1)} %param.9) | copy-start | bytes 393220
  34.0 209.9 %all-reduce.8.cloned.1.call-start = ((), (), s32[]{:S(2)}) async-start(), calls=%async_computation.3 | async-start | bytes 131072 | tf_op jit(solution)/shard_map/psum | solution.py:42
  132.1 111.7 %copy-start.1 = (f32[32,512]{1,0:T(8,128)S(1)}, f32[32,512]{1,0:T(8,128)}, u32[]{:S(2)}) copy-start(f32[32,512]{1,0:T(8,128)} %all-reduce.6.cloned.1.call-done) | copy-start | bytes 196612
  147.8 171.5 %all-reduce.12.cloned.1.call-start = ((), (), s32[]{:S(2)}) async-start(), calls=%async_computation.7 | async-start | bytes 4194304 | tf_op jit(solution)/shard_map/psum | solution.py:53
  149.2 111.4 %copy-start.4 = (s32[512]{0:T(512)S(1)}, s32[512]{0:T(512)}, u32[]{:S(2)}) copy-start(s32[512]{0:T(512)} %param.11) | copy-start | bytes 6148
  259.4 185.7 %copy-start.5 = (f32[512,16]{0,1:T(8,128)S(1)}, f32[512,16]{0,1:T(8,128)}, u32[]{:S(2)}) copy-start(f32[512,16]{0,1:T(8,128)} %param.10) | copy-start | bytes 98308
  260.5 274.5 %reduce-scatter.7.cloned.1.call-start = ((), (), s32[]{:S(2)}) async-start(), calls=%async_computation.6 | async-start | bytes 270336
  445.0 8.4 %copy-start.3 = (bf16[512,128]{1,0:T(8,128)(2,1)S(1)}, bf16[512,128]{1,0:T(8,128)(2,1)}, u32[]{:S(2)}) copy-start(bf16[512,128]{1,0:T(8,128)(2,1)} %param.9) | copy-start | bytes 393220
  445.0 133.6 %all-reduce.10.cloned.1.call-start = ((), (), s32[]{:S(2)}) async-start(), calls=%async_computation.5 | async-start | bytes 524288 | tf_op jit(solution)/shard_map/psum | solution.py:58
  453.4 211.5 %reduce-scatter.5.cloned.1.call-start = ((), (), s32[]{:S(2)}) async-start(), calls=%async_computation.4 | async-start | bytes 4325376 | tf_op jit(solution)/shard_map/reduce_scatter | solution.py:64
Sparse Core Ops, SparseCore 0:
  34.1 97.9 all-reduce.5
  148.0 95.8 all-reduce.7
  260.6 58.6 all-reduce.11
  445.1 89.8 reduce-scatter.6
  537.2 41.3 all-reduce.9
  582.1 82.6 reduce-scatter.4
where the time goes:
time: 675 us; the launch traced here: 673 us
  waiting for transfers between devices  439 us (65%)
  blocking collectives  112 us (17%)
  matrix products  54.5 us (8%)
  other arithmetic  50 us (7%)
  between operations  14.2 us (2%)
    psum x1, waiting for transfers between devices, per_device(): row_total = lax.psum(local_total, 'keys')  94.7 us
    pmax x1, waiting for transfers between devices, per_device(): row_max = lax.pmax(local_max, 'keys')  89.9 us
    reduce_scatter x1, waiting for transfers between devices, per_device(): lax.psum_scatter(query_part, 'keys', scatter_dimension=0, tiled=True)  84.5 us
    unnamed x7, waiting for transfers between devices  69.3 us
    psum x1, waiting for transfers between devices, per_device(): target, logits = lax.psum((target_part, logit_part), 'heads')  58.7 us
    psum x1, blocking collectives, logit_gradient(): logit_total = lax.psum(local_expsum, 'keys')  56.4 us
    pmax x1, blocking collectives, logit_gradient(): logit_max = lax.pmax(logit_local, 'keys')  55.5 us
    psum x1, waiting for transfers between devices, per_device(): grad_index_keys = lax.psum(key_part, 'heads') * index_scale  42.2 us
  transfers between devices with their start and end apart: 6, of which 6 were waited for; matrix products, arithmetic and copies ran while one was open for 5% of the time, Pallas kernels for 0%

commit v1 on v0

v1 whole, which is shorter than its diff:
```python
import functools

import jax
import jax.numpy as jnp
from jax import lax
from jax.experimental import pallas as pl
from jax.experimental.pallas import tpu as pltpu
from jax.sharding import PartitionSpec as P

H = 128
DL = 576
HI = 64
DI = 128
NK = 32
NX = 4
NY = 4
NZ = 4
C = 4
T = 128
S = 512
SQ = S // NX
HL = H // NX
JL = HI // NX
LOG2E = 1.4426950408889634
K2 = 2.0 * DL ** (-0.5) * LOG2E
IS = DI ** (-0.5)
HS = HI ** (-0.5)
NEG = -1e30
BIG = 3e38
MESH = pl.DeviceIdType.MESH
F32 = jnp.float32
BF16 = jnp.bfloat16


def twice(a):
    return jnp.concatenate([a, a], axis=1)


def kernel(
    q_hbm, k_ref, iq_ref, ik_ref, w_ref, lim_ref,
    oq_ref, ow_ref, ok_ref,
    qb, p_ref, s_ref, m_ref, cap_ref, ikt_ref, wj_ref, gj_ref,
    lo_ref, lr_ref, lq_ref, ls_ref, xr_ref, lk_ref, kr_ref, lf_ref,
    st_ref, sr_ref, rr_ref, gl_ref, cc_ref,
    tg_ref, tr_ref, lg_ref, gw_ref, ka_ref,
    qp_ref, pr_ref, qs_ref, zr_ref, ys_ref, yr_ref, kx_ref, ko_ref,
    qsem,
    lo_s, lo_r, xs_s, xs_r, kk_s, kk_r, ss_s, ss_r, gl_s, gl_r, tg_s, tg_r,
    lg_s, lg_r, pp_s, pp_r, zz_s, zz_r, yy_s, yy_r, kx_s, kx_r, ko_s, ko_r,
):
    k = lax.axis_index("keys")
    x = lax.axis_index("heads")
    core = lax.rem(k, 2)
    z = lax.rem(k // 2, NZ)
    y = k // (2 * NZ)
    myq = pl.multiple_of(x * SQ, SQ)

    def q_copy(c):
        return pltpu.make_async_copy(
            q_hbm.at[:, :, pl.ds(c * T, T)], qb.at[c % 2], qsem.at[c % 2]
        )

    def send(src, dst, ssem, rsem, kd, xd):
        pltpu.make_async_remote_copy(
            src_ref=src, dst_ref=dst, send_sem=ssem, recv_sem=rsem,
            device_id=(kd, xd), device_id_type=MESH,
        ).start()

    def wait(ref, sem):
        pltpu.make_async_copy(ref, ref, sem).wait()

    def to_keys(fn):
        def body(r, carry):
            fn(r, lax.rem(k + r, NK))
            return carry

        lax.fori_loop(1, NK, body, 0)

    def to_heads(fn):
        for r in range(1, NX):
            fn(r, lax.rem(x + r, NX))

    q_copy(0).start()
    barrier = pltpu.get_barrier_semaphore()
    to_keys(lambda r, o: pl.semaphore_signal(barrier, inc=1, device_id=(o, x), device_id_type=MESH))
    to_heads(lambda r, o: pl.semaphore_signal(barrier, inc=1, device_id=(k, o), device_id_type=MESH))

    pos = k * S + lax.broadcasted_iota(jnp.int32, (S, T), 0)
    for c in range(C):
        cap_ref[c] = jnp.where(pos <= lim_ref[0:1, c * T : (c + 1) * T], BIG, NEG)
    for j in range(JL):
        wj_ref[j] = w_ref[j : j + 1, :]
    ikt_ref[...] = ik_ref[...].astype(F32).T.astype(BF16)
    pl.semaphore_wait(barrier, NK - 1 + NX - 1)

    def index_dots(c, jj):
        pair = iq_ref[pl.ds(2 * jj, 2), c * T : (c + 1) * T, :].reshape(2 * T, DI)
        dots = lax.dot_general(
            ik_ref[...], pair, (((1,), (1,)), ((), ())), preferred_element_type=F32
        )
        row = jnp.concatenate(
            [wj_ref[2 * jj, :, c * T : (c + 1) * T], wj_ref[2 * jj + 1, :, c * T : (c + 1) * T]],
            axis=1,
        )
        return pair, dots, row

    def index_forward(c):
        lo_ref[c] = jnp.zeros((S, T), F32)

        def body(jj, carry):
            _, dots, row = index_dots(c, jj)
            term = jnp.maximum(dots, 0.0) * (row * (IS * HS))
            lo_ref[c] += term[:, :T] + term[:, T:]
            return carry

        lax.fori_loop(0, JL // 2, body, 0)
        to_heads(lambda r, o: send(
            lo_ref.at[c, pl.ds(pl.multiple_of(o * SQ, SQ), SQ)], lr_ref.at[c, r - 1],
            lo_s.at[c], lo_r.at[c], k, o))

    def scores(c):
        q_copy(c).wait()
        if c + 1 < C:
            q_copy(c + 1).start()
        slot = c % 2
        ps = c % 3

        def dots(i, u):
            h = 2 * i
            qt = jnp.concatenate([qb[slot, h], qb[slot, h + 1]], axis=1)
            s = jnp.dot(k_ref[...], qt, preferred_element_type=F32)
            s = jnp.minimum(s, twice(cap_ref[c]))
            s_ref[u] = s
            m = jnp.max(s, axis=0, keepdims=True)
            m_ref[u] = m
            st_ref[c, h, 0:1, :] = m[:, :T]
            st_ref[c, h + 1, 0:1, :] = m[:, T:]

        def soft(i, u):
            h = 2 * i
            p = jnp.exp2((s_ref[u] - m_ref[u]) * K2)
            l = jnp.sum(p, axis=0, keepdims=True)
            p_ref[ps, h] = p[:, :T]
            p_ref[ps, h + 1] = p[:, T:]
            st_ref[c, h, 1:2, :] = l[:, :T]
            st_ref[c, h + 1, 1:2, :] = l[:, T:]

        dots(0, 0)

        def body(i, carry):
            dots(2 * i + 1, 1)
            soft(2 * i, 0)
            dots(jnp.minimum(2 * i + 2, HL // 2 - 1), 0)
            soft(2 * i + 1, 1)
            return carry

        lax.fori_loop(0, HL // 4, body, 0)
        to_keys(lambda r, o: send(
            st_ref.at[c, o], sr_ref.at[c, r - 1], ss_s.at[c], ss_r.at[c], o, x))

    def combine(c):
        wait(sr_ref.at[c], ss_r.at[c])
        own = st_ref[c, k]
        ms = sr_ref[c, :, 0, :]
        sums = sr_ref[c, :, 1, :]
        m = jnp.maximum(own[0:1], jnp.max(ms, axis=0, keepdims=True))
        total = own[1:2] * jnp.exp2((own[0:1] - m) * K2) + jnp.sum(
            sums * jnp.exp2((ms - m) * K2), axis=0, keepdims=True
        )
        rr_ref[c, 0:1, :] = m
        rr_ref[c, 1:2, :] = 1.0 / (total * H)
        gl_ref[c, k] = rr_ref[c]
        to_keys(lambda r, o: send(rr_ref.at[c], gl_ref.at[c, k], gl_s.at[c], gl_r.at[c], o, x))

    def logit_stats():
        for c in range(C):
            wait(lr_ref.at[c], lo_r.at[c])
            v = lo_ref[c, pl.ds(myq, SQ), :] + lr_ref[c, 0] + lr_ref[c, 1] + lr_ref[c, 2]
            v = jnp.minimum(v, cap_ref[c, pl.ds(myq, SQ), :])
            lq_ref[c] = v
            m = jnp.max(v, axis=0, keepdims=True)
            ls_ref[c, 0:1, :] = m
            ls_ref[c, 1:2, :] = jnp.sum(jnp.exp(v - m), axis=0, keepdims=True)
        to_heads(lambda r, o: send(ls_ref, xr_ref.at[r - 1], xs_s, xs_r, k, o))

    def logit_stats_heads():
        wait(xr_ref, xs_r)
        for c in range(C):
            ms = [ls_ref[c, 0:1, :]] + [xr_ref[r, c, 0:1, :] for r in range(NX - 1)]
            ts = [ls_ref[c, 1:2, :]] + [xr_ref[r, c, 1:2, :] for r in range(NX - 1)]
            m = functools.reduce(jnp.maximum, ms)
            lk_ref[c, 0:1, :] = m
            lk_ref[c, 1:2, :] = sum(t * jnp.exp(a - m) for a, t in zip(ms, ts))
        to_keys(lambda r, o: send(lk_ref, kr_ref.at[r - 1], kk_s, kk_r, o, x))

    def logit_stats_keys():
        wait(kr_ref, kk_r)
        for c in range(C):
            own_m, own_t = lk_ref[c, 0:1, :], lk_ref[c, 1:2, :]
            ms = kr_ref[:, c, 0, :]
            ts = kr_ref[:, c, 1, :]
            m = jnp.maximum(own_m, jnp.max(ms, axis=0, keepdims=True))
            lf_ref[c, 0:1, :] = m
            lf_ref[c, 1:2, :] = own_t * jnp.exp(own_m - m) + jnp.sum(
                ts * jnp.exp(ms - m), axis=0, keepdims=True
            )

    def target(c):
        wait(gl_ref.at[c, pl.ds(0, NK - 1)], gl_r.at[c])
        cc_ref[...] = jnp.exp2((st_ref[c, :, 0, :] - gl_ref[c, :, 0, :]) * K2) * gl_ref[c, :, 1, :]
        ps = c % 3
        rows = 64

        def body(b, carry):
            at = pl.ds(pl.multiple_of(b * rows, rows), rows)
            acc = p_ref[ps, 0, at, :] * cc_ref[0:1, :]
            for h in range(1, HL):
                acc += p_ref[ps, h, at, :] * cc_ref[h : h + 1, :]
            tg_ref[c, at, :] = acc
            return carry

        lax.fori_loop(0, S // rows, body, 0)
        to_heads(lambda r, o: send(
            tg_ref.at[c, pl.ds(pl.multiple_of(o * SQ, SQ), SQ)], tr_ref.at[c, r - 1],
            tg_s.at[c], tg_r.at[c], k, o))

    def logit_grad(c):
        wait(tr_ref.at[c], tg_r.at[c])
        t = tg_ref[c, pl.ds(myq, SQ), :] + tr_ref[c, 0] + tr_ref[c, 1] + tr_ref[c, 2]
        v = lq_ref[c]
        probs = jnp.where(
            cap_ref[c, pl.ds(myq, SQ), :] > 0, jnp.exp(v - lf_ref[c, 0:1, :]), 0.0
        ) / lf_ref[c, 1:2, :]
        span = (lim_ref[0:1, c * T : (c + 1) * T] + 1).astype(F32)
        lg_ref[c, pl.ds(myq, SQ), :] = (probs - t) * span
        to_heads(lambda r, o: send(
            lg_ref.at[c, pl.ds(myq, SQ)], lg_ref.at[c, pl.ds(myq, SQ)],
            lg_s.at[c], lg_r.at[c], k, o))

    def grads(c):
        wait(tr_ref.at[c], lg_r.at[c])

        def body(jj, carry):
            pair, dots, row = index_dots(c, jj)
            lg = twice(lg_ref[c])
            gw = jnp.sum(lg * jnp.maximum(dots, 0.0), axis=0, keepdims=True) * (IS * HS)
            gj_ref[2 * jj] = gw[:, :T]
            gj_ref[2 * jj + 1] = gw[:, T:]
            g = jnp.where(dots > 0, lg * (row * HS), 0.0).astype(BF16)
            qpt = jnp.dot(ikt_ref[...], g, preferred_element_type=F32)
            qp = qpt.T * IS
            for u in range(2):
                for zz in range(NZ):
                    for cr in range(2):
                        at = u * T + (zz * 2 + cr) * 16
                        qp_ref[c, cr, zz, 2 * jj + u] = qp[at : at + 16]
            part = jnp.dot(g, pair, preferred_element_type=F32)
            ka_ref[...] += part
            return carry

        lax.fori_loop(0, JL // 2, body, 0)
        for j in range(JL):
            gw_ref[j : j + 1, :] = gj_ref[j]
        gwt = gw_ref[...].T
        for zz in range(NZ):
            for cr in range(2):
                at = (zz * 2 + cr) * 16
                qp_ref[c, cr, zz, JL] = gwt[at : at + 16]
        send(qp_ref.at[c, 1 - core], pr_ref.at[c], pp_s.at[c], pp_r.at[c], k + 1 - 2 * core, x)

    def pair_sum(c):
        wait(pr_ref.at[c], pp_r.at[c])
        for zz in range(NZ):
            qs_ref[c, zz] = qp_ref[c, core, zz] + pr_ref[c, zz]
        for dz in range(1, NZ):
            zd = lax.rem(z + dz, NZ)
            send(qs_ref.at[c, zd], zr_ref.at[c, dz - 1], zz_s.at[c], zz_r.at[c], (y * NZ + zd) * 2 + core, x)

    def plane_sum(c):
        wait(zr_ref.at[c], zz_r.at[c])
        ys_ref[c] = qs_ref[c, z] + zr_ref[c, 0] + zr_ref[c, 1] + zr_ref[c, 2]
        slot = lax.rem(y - c + NY - 1, NY)

        @pl.when(y != c)
        def _():
            send(ys_ref.at[c], yr_ref.at[slot], yy_s.at[c], yy_r, (c * NZ + z) * 2 + core, x)

    def key_send():
        to_heads(lambda r, o: send(
            ka_ref.at[pl.ds(pl.multiple_of(o * SQ, SQ), SQ)], kx_ref.at[r - 1], kx_s, kx_r, k, o))

    def key_sum():
        wait(kx_ref, kx_r)
        ko_ref[pl.ds(myq, SQ), :] = (
            ka_ref[pl.ds(myq, SQ), :] + kx_ref[0] + kx_ref[1] + kx_ref[2]
        ) * IS
        to_heads(lambda r, o: send(
            ko_ref.at[pl.ds(myq, SQ)], ko_ref.at[pl.ds(myq, SQ)], ko_s, ko_r, k, o))

    gw_ref[...] = jnp.zeros_like(gw_ref)
    ka_ref[...] = jnp.zeros_like(ka_ref)
    for c in range(C):
        index_forward(c)
    scores(0)
    logit_stats()
    scores(1)
    combine(0)
    logit_stats_heads()
    scores(2)
    combine(1)
    target(0)
    logit_stats_keys()
    scores(3)
    combine(2)
    logit_grad(0)
    target(1)
    grads(0)
    combine(3)
    logit_grad(1)
    target(2)
    pair_sum(0)
    grads(1)
    logit_grad(2)
    target(3)
    plane_sum(0)
    pair_sum(1)
    grads(2)
    logit_grad(3)
    plane_sum(1)
    pair_sum(2)
    grads(3)
    key_send()
    plane_sum(2)
    pair_sum(3)
    key_sum()
    plane_sum(3)
    wait(yr_ref, yy_r)
    mine = ys_ref[y] + yr_ref[0] + yr_ref[1] + yr_ref[2]
    oq_ref[...] = mine[:JL]
    ow_ref[...] = mine[JL]
    wait(kx_ref, ko_r)
    ok_ref[...] = ko_ref[...]

    wait(xr_ref, xs_s)
    wait(kr_ref, kk_s)
    wait(kx_ref, kx_s)
    wait(kx_ref, ko_s)
    for c in range(C):
        wait(lr_ref.at[c], lo_s.at[c])
        wait(sr_ref.at[c], ss_s.at[c])
        wait(sr_ref.at[c], gl_s.at[c])
        wait(tr_ref.at[c], tg_s.at[c])
        wait(tr_ref.at[c], lg_s.at[c])
        wait(pr_ref.at[c], pp_s.at[c])
        wait(zr_ref.at[c], zz_s.at[c])

        @pl.when(y != c)
        def _():
            wait(ys_ref.at[c], yy_s.at[c])


def per_device(main_query, latent_keys, index_query, index_keys, index_weights, query_limit):
    vm = pl.BlockSpec(memory_space=pltpu.VMEM)
    dma = pltpu.SemaphoreType.DMA
    oq, ow, ok = pl.pallas_call(
        kernel,
        out_shape=(
            jax.ShapeDtypeStruct((JL, 16, DI), F32),
            jax.ShapeDtypeStruct((16, DI), F32),
            jax.ShapeDtypeStruct((S, DI), F32),
        ),
        in_specs=[pl.BlockSpec(memory_space=pl.ANY)] + [vm] * 5,
        out_specs=(vm, vm, vm),
        scratch_shapes=[
            pltpu.VMEM((2, HL, DL, T), BF16),
            pltpu.VMEM((3, HL, S, T), F32),
            pltpu.VMEM((2, S, 2 * T), F32),
            pltpu.VMEM((2, 1, 2 * T), F32),
            pltpu.VMEM((C, S, T), F32),
            pltpu.VMEM((DI, S), BF16),
            pltpu.VMEM((JL, 1, C * T), F32),
            pltpu.VMEM((JL, 1, T), F32),
            pltpu.VMEM((C, S, T), F32),
            pltpu.VMEM((C, NX - 1, SQ, T), F32),
            pltpu.VMEM((C, SQ, T), F32),
            pltpu.VMEM((C, 2, T), F32),
            pltpu.VMEM((NX - 1, C, 2, T), F32),
            pltpu.VMEM((C, 2, T), F32),
            pltpu.VMEM((NK - 1, C, 2, T), F32),
            pltpu.VMEM((C, 2, T), F32),
            pltpu.VMEM((C, HL, 2, T), F32),
            pltpu.VMEM((C, NK - 1, 2, T), F32),
            pltpu.VMEM((C, 2, T), F32),
            pltpu.VMEM((C, HL, 2, T), F32),
            pltpu.VMEM((HL, T), F32),
            pltpu.VMEM((C, S, T), F32),
            pltpu.VMEM((C, NX - 1, SQ, T), F32),
            pltpu.VMEM((C, S, T), F32),
            pltpu.VMEM((DI, T), F32),
            pltpu.VMEM((S, DI), F32),
            pltpu.VMEM((C, 2, NZ, JL + 1, 16, DI), F32),
            pltpu.VMEM((C, NZ, JL + 1, 16, DI), F32),
            pltpu.VMEM((C, NZ, JL + 1, 16, DI), F32),
            pltpu.VMEM((C, NZ - 1, JL + 1, 16, DI), F32),
            pltpu.VMEM((C, JL + 1, 16, DI), F32),
            pltpu.VMEM((NY - 1, JL + 1, 16, DI), F32),
            pltpu.VMEM((NX - 1, SQ, DI), F32),
            pltpu.VMEM((S, DI), F32),
            dma((2,)),
            dma((C,)), dma((C,)), dma, dma, dma, dma, dma((C,)), dma((C,)), dma((C,)), dma((C,)),
            dma((C,)), dma((C,)), dma((C,)), dma((C,)), dma((C,)), dma((C,)), dma((C,)), dma((C,)),
            dma((C,)), dma, dma, dma, dma, dma,
        ],
        compiler_params=pltpu.CompilerParams(
            collective_id=0, has_side_effects=True, vmem_limit_bytes=67043328
        ),
    )(
        jnp.transpose(main_query, (1, 2, 0)),
        latent_keys,
        jnp.transpose(index_query, (1, 0, 2)),
        index_keys,
        index_weights.T,
        query_limit.reshape(1, -1),
    )
    return jnp.transpose(oq, (1, 0, 2)), ow[:, :JL], ok


def solution(mesh):
    in_specs = (
        P(None, "heads", None),
        P("keys", None),
        P(None, "heads", None),
        P("keys", None),
        P(None, "heads"),
        P(),
    )
    out_specs = (P("keys", "heads", None), P("keys", "heads"), P("keys", None))
    return jax.shard_map(
        per_device, mesh=mesh, in_specs=in_specs, out_specs=out_specs, check_vma=False
    )
```

time: 675 us -> 116 us (0.17)
  waiting for transfers between devices: 439 us -> 0 us
  blocking collectives: 112 us -> 0 us
  Pallas kernels: 0 us -> 105 us
  matrix products: 54.5 us -> 0 us
  other arithmetic: 50 us -> 0 us
  between operations: 14.2 us -> 0.64 us
  local copies, waits for them, and re-layouts: 3.01 us -> 10.2 us
    psum x3 -> x0, waiting for transfers between devices: 196 us -> none  [the longest x1 94.7 us: per_device(): row_total = lax.psum(local_total, 'keys')]
    pallas_call x0 -> x1, Pallas kernels: none -> 105 us  [per_device(): pl.pallas_call(kernel, out_shape=(jax.ShapeDtypeStruct((JL, 16, DI), F32)...]
    pmax x1 -> x0, waiting for transfers between devices: 89.9 us -> none  [per_device(): row_max = lax.pmax(local_max, 'keys')]
    reduce_scatter x1 -> x0, waiting for transfers between devices: 84.5 us -> none  [per_device(): lax.psum_scatter(query_part, 'keys', scatter_dimension=0, tiled=True)]
    unnamed x7 -> x0, waiting for transfers between devices: 69.3 us -> none
    psum x1 -> x0, blocking collectives: 56.4 us -> none  [logit_gradient(): logit_total = lax.psum(local_expsum, 'keys')]
    pmax x1 -> x0, blocking collectives: 55.5 us -> none  [logit_gradient(): logit_max = lax.pmax(logit_local, 'keys')]
    dot_general x4 -> x0, matrix products: 54.5 us -> none  [the longest x1 25.7 us: per_device(): jnp.einsum('thd,sd->hts', main_query, latent_keys, preferred_element_type...]
  transfers between devices with their start and end apart: 6 -> 0, of which waited for: 6 -> 0; matrix products, arithmetic and copies ran while one was open for 5% -> 0% of each run, Pallas kernels for 0% -> 0%
where the time goes in v1:
time: 116 us; the launch traced here: 115 us
  Pallas kernels  105 us (91%)
  local copies, waits for them, and re-layouts  10.2 us (9%)
    pallas_call x1, Pallas kernels, per_device(): pl.pallas_call(kernel, out_shape=(jax.ShapeDtypeStruct((JL, 16, DI), F32)...  105 us
    unnamed x5, local copies, waits for them, and re-layouts  10.2 us

profile of v1, /device:TPU:24, one launch (start us, length us, event | category | flops | bytes accessed | tf_op | source)
XLA Modules:
  0.0 115.4 jit_solution(15394008448026425367)
XLA Ops:
  0.6 2.2 %copy.10.k_ref = bf16[512,576]{1,0:T(8,128)(2,1)} copy(bf16[512,576]{0,1:T(8,128)(2,1)} %param.7) | data formatting | bytes 1179648 | tf_op args[1]
  2.8 3.5 %copy.13 = bf16[512,16,128]{2,0,1:T(8,128)(2,1)} copy(bf16[512,16,128]{2,1,0:T(8,128)(2,1)} %param.8) | data formatting | bytes 4194304 | tf_op args[2]
  6.3 104.6 %shard_map.85 = (f32[16,16,128]{2,1,0:T(8,128)}, f32[16,128]{1,0:T(8,128)}, f32[512,128]{1,0:T(8,128)}) custom-call(bf16[32,576,512]{2,1,0:T(8,128)(2,1)} %bitcast.8, bf16[512,576]{1,0:T(8,128)(2,1)} %copy.10.k_ref, bf16[16,512,128]{2,1,0:T(8,128)(2,1)} %bitcast.9, bf16[512,128]{1,0:T(8,128)(2,1)} %ik_ref.1, f32[16,512]{1,0:T(8,128)} %bitcast.11, ...), custom_call_target="tpu_custom_call" | custom-call | tf_op jit(solution)/shard_map/pallas_call | solution.py:365
  110.9 1.6 %copy.11 = f32[16,16,128]{2,1,0:T(8,128)} copy(f32[16,16,128]{2,0,1:T(8,128)} %bitcast.10) | data formatting | bytes 262144
  112.5 1.3 %copy.16 = f32[16,16]{1,0:T(8,128)} copy(f32[16,16]{1,0:T(8,128)} %bitcast.12) | data formatting | bytes 2048
  113.8 1.7 %copy.17 = f32[512,128]{1,0:T(8,128)} copy(f32[512,128]{1,0:T(8,128)} %get-tuple-element.17) | data formatting | bytes 524288

commit v2 on v1

--- a/solution.py
+++ b/solution.py
@@ -37,14 +37,15 @@
 
 
 def kernel(
-    q_hbm, k_ref, iq_ref, ik_ref, w_ref, lim_ref,
+    q_hbm, kt_hbm, iq_hbm, ik_hbm, w_ref, lim_ref,
     oq_ref, ow_ref, ok_ref,
     qb, p_ref, s_ref, m_ref, cap_ref, ikt_ref, wj_ref, gj_ref,
+    kt_ref, k_ref, iqr_ref, tmp_ref, iq_ref, ik_ref, ga_ref, gb_ref,
     lo_ref, lr_ref, lq_ref, ls_ref, xr_ref, lk_ref, kr_ref, lf_ref,
     st_ref, sr_ref, rr_ref, gl_ref, cc_ref,
     tg_ref, tr_ref, lg_ref, gw_ref, ka_ref,
     qp_ref, pr_ref, qs_ref, zr_ref, ys_ref, yr_ref, kx_ref, ko_ref,
-    qsem,
+    qsem, isem,
     lo_s, lo_r, xs_s, xs_r, kk_s, kk_r, ss_s, ss_r, gl_s, gl_r, tg_s, tg_r,
     lg_s, lg_r, pp_s, pp_r, zz_s, zz_r, yy_s, yy_r, kx_s, kx_r, ko_s, ko_r,
 ):
@@ -80,6 +81,12 @@
         for r in range(1, NX):
             fn(r, lax.rem(x + r, NX))
 
+    loads = [
+        pltpu.make_async_copy(a, b, isem.at[n])
+        for n, (a, b) in enumerate(((iq_hbm, iqr_ref), (ik_hbm, ik_ref), (kt_hbm, kt_ref)))
+    ]
+    for load in loads:
+        load.start()
     q_copy(0).start()
     barrier = pltpu.get_barrier_semaphore()
     to_keys(lambda r, o: pl.semaphore_signal(barrier, inc=1, device_id=(o, x), device_id_type=MESH))
@@ -90,36 +97,66 @@
         cap_ref[c] = jnp.where(pos <= lim_ref[0:1, c * T : (c + 1) * T], BIG, NEG)
     for j in range(JL):
         wj_ref[j] = w_ref[j : j + 1, :]
+    loads[1].wait()
     ikt_ref[...] = ik_ref[...].astype(F32).T.astype(BF16)
-    pl.semaphore_wait(barrier, NK - 1 + NX - 1)
-
-    def index_dots(c, jj):
-        pair = iq_ref[pl.ds(2 * jj, 2), c * T : (c + 1) * T, :].reshape(2 * T, DI)
-        dots = lax.dot_general(
-            ik_ref[...], pair, (((1,), (1,)), ((), ())), preferred_element_type=F32
-        )
-        row = jnp.concatenate(
+    loads[0].wait()
+    for c in range(C):
+        tmp_ref[...] = iqr_ref[c * T : (c + 1) * T].astype(F32).reshape(T * JL, DI)
+        for j in range(JL):
+            iq_ref[j, c * T : (c + 1) * T] = tmp_ref[pl.ds(j, T, stride=JL), :].astype(BF16)
+
+    def rows_of(c, jj):
+        return jnp.concatenate(
             [wj_ref[2 * jj, :, c * T : (c + 1) * T], wj_ref[2 * jj + 1, :, c * T : (c + 1) * T]],
             axis=1,
         )
-        return pair, dots, row
+
+    def index_dots(c, jj, u):
+        pair = iq_ref[pl.ds(2 * jj, 2), c * T : (c + 1) * T, :].reshape(2 * T, DI)
+        s_ref[u] = lax.dot_general(
+            ik_ref[...], pair, (((1,), (1,)), ((), ())), preferred_element_type=F32
+        )
 
     def index_forward(c):
         lo_ref[c] = jnp.zeros((S, T), F32)
 
-        def body(jj, carry):
-            _, dots, row = index_dots(c, jj)
-            term = jnp.maximum(dots, 0.0) * (row * (IS * HS))
-            lo_ref[c] += term[:, :T] + term[:, T:]
+        def add(jj, u):
+            total = None
+            for v in range(2):
+                row = rows_of(c, jj + v) * (IS * HS)
+                term = jnp.maximum(s_ref[u + v], 0.0) * row
+                part = term[:, :T] + term[:, T:]
+                total = part if total is None else total + part
+            lo_ref[c] += total
+
+        def two(jj, u):
+            index_dots(c, jj, u)
+            index_dots(c, jj + 1, u + 1)
+
+        two(0, 0)
+
+        def body(i, carry):
+            two(4 * i + 2, 2)
+            add(4 * i, 0)
+            two(jnp.minimum(4 * i + 4, JL // 2 - 2), 0)
+            add(4 * i + 2, 2)
             return carry
 
-        lax.fori_loop(0, JL // 2, body, 0)
+        lax.fori_loop(0, JL // 8, body, 0)
+        if c == 0:
+            pl.semaphore_wait(barrier, NK - 1 + NX - 1)
         to_heads(lambda r, o: send(
             lo_ref.at[c, pl.ds(pl.multiple_of(o * SQ, SQ), SQ)], lr_ref.at[c, r - 1],
             lo_s.at[c], lo_r.at[c], k, o))
 
     def scores(c):
         q_copy(c).wait()
+        if c == 0:
+            loads[2].wait()
+            for b in range(S // 128):
+                k_ref[b * 128 : (b + 1) * 128, :] = (
+                    kt_ref[:, b * 128 : (b + 1) * 128].astype(F32).T.astype(BF16)
+                )
         if c + 1 < C:
             q_copy(c + 1).start()
         slot = c % 2
@@ -240,25 +277,41 @@
     def grads(c):
         wait(tr_ref.at[c], lg_r.at[c])
 
-        def body(jj, carry):
-            pair, dots, row = index_dots(c, jj)
+        def gate(jj, u, out, at):
+            dots = s_ref[u]
             lg = twice(lg_ref[c])
             gw = jnp.sum(lg * jnp.maximum(dots, 0.0), axis=0, keepdims=True) * (IS * HS)
             gj_ref[2 * jj] = gw[:, :T]
             gj_ref[2 * jj + 1] = gw[:, T:]
-            g = jnp.where(dots > 0, lg * (row * HS), 0.0).astype(BF16)
-            qpt = jnp.dot(ikt_ref[...], g, preferred_element_type=F32)
-            qp = qpt.T * IS
-            for u in range(2):
+            g = jnp.where(dots > 0, lg * (rows_of(c, jj) * HS), 0.0)
+            out[:, at : at + 2 * T] = g.astype(BF16)
+
+        def products(g_ref, j0):
+            g = g_ref[...]
+            four = iq_ref[pl.ds(j0, 4), c * T : (c + 1) * T, :].reshape(4 * T, DI)
+            qpt = jnp.dot(ikt_ref[...], g, preferred_element_type=F32) * IS
+            for u in range(4):
+                qp = qpt[:, u * T : (u + 1) * T].T
                 for zz in range(NZ):
                     for cr in range(2):
-                        at = u * T + (zz * 2 + cr) * 16
-                        qp_ref[c, cr, zz, 2 * jj + u] = qp[at : at + 16]
-            part = jnp.dot(g, pair, preferred_element_type=F32)
-            ka_ref[...] += part
+                        at = (zz * 2 + cr) * 16
+                        qp_ref[c, cr, zz, j0 + u] = qp[at : at + 16]
+            ka_ref[...] += jnp.dot(g, four, preferred_element_type=F32)
+
+        gb_ref[...] = jnp.zeros_like(gb_ref)
+        index_dots(c, 0, 0)
+
+        def body(i, carry):
+            products(gb_ref, jnp.maximum(8 * i - 4, 0))
+            for u in range(4):
+                index_dots(c, jnp.minimum(4 * i + u + 1, JL // 2 - 1), (u + 1) % 2)
+                gate(4 * i + u, u % 2, ga_ref if u < 2 else gb_ref, (u % 2) * 2 * T)
+                if u == 1:
+                    products(ga_ref, 8 * i)
             return carry
 
-        lax.fori_loop(0, JL // 2, body, 0)
+        lax.fori_loop(0, JL // 8, body, 0)
+        products(gb_ref, JL - 4)
         for j in range(JL):
             gw_ref[j : j + 1, :] = gj_ref[j]
         gwt = gw_ref[...].T
@@ -359,6 +412,13 @@
             wait(ys_ref.at[c], yy_s.at[c])
 
 
+def finish(oq_ref, ow_ref, ok_ref, q_ref, w_ref, k_ref):
+    for j in range(JL):
+        q_ref[:, j, :] = oq_ref[j]
+    w_ref[...] = ow_ref[:, :JL]
+    k_ref[...] = ok_ref[...]
+
+
 def per_device(main_query, latent_keys, index_query, index_keys, index_weights, query_limit):
     vm = pl.BlockSpec(memory_space=pltpu.VMEM)
     dma = pltpu.SemaphoreType.DMA
@@ -369,17 +429,25 @@
             jax.ShapeDtypeStruct((16, DI), F32),
             jax.ShapeDtypeStruct((S, DI), F32),
         ),
-        in_specs=[pl.BlockSpec(memory_space=pl.ANY)] + [vm] * 5,
+        in_specs=[pl.BlockSpec(memory_space=pl.ANY)] * 4 + [vm] * 2,
         out_specs=(vm, vm, vm),
         scratch_shapes=[
             pltpu.VMEM((2, HL, DL, T), BF16),
             pltpu.VMEM((3, HL, S, T), F32),
-            pltpu.VMEM((2, S, 2 * T), F32),
+            pltpu.VMEM((4, S, 2 * T), F32),
             pltpu.VMEM((2, 1, 2 * T), F32),
             pltpu.VMEM((C, S, T), F32),
             pltpu.VMEM((DI, S), BF16),
             pltpu.VMEM((JL, 1, C * T), F32),
             pltpu.VMEM((JL, 1, T), F32),
+            pltpu.VMEM((DL, S), BF16),
+            pltpu.VMEM((S, DL), BF16),
+            pltpu.VMEM((C * T, JL, DI), BF16),
+            pltpu.VMEM((T * JL, DI), F32),
+            pltpu.VMEM((JL, C * T, DI), BF16),
+            pltpu.VMEM((S, DI), BF16),
+            pltpu.VMEM((S, 4 * T), BF16),
+            pltpu.VMEM((S, 4 * T), BF16),
             pltpu.VMEM((C, S, T), F32),
             pltpu.VMEM((C, NX - 1, SQ, T), F32),
             pltpu.VMEM((C, SQ, T), F32),
@@ -406,7 +474,7 @@
             pltpu.VMEM((NY - 1, JL + 1, 16, DI), F32),
             pltpu.VMEM((NX - 1, SQ, DI), F32),
             pltpu.VMEM((S, DI), F32),
-            dma((2,)),
+            dma((2,)), dma((3,)),
             dma((C,)), dma((C,)), dma, dma, dma, dma, dma((C,)), dma((C,)), dma((C,)), dma((C,)),
             dma((C,)), dma((C,)), dma((C,)), dma((C,)), dma((C,)), dma((C,)), dma((C,)), dma((C,)),
             dma((C,)), dma, dma, dma, dma, dma,
@@ -416,13 +484,22 @@
         ),
     )(
         jnp.transpose(main_query, (1, 2, 0)),
-        latent_keys,
-        jnp.transpose(index_query, (1, 0, 2)),
+        latent_keys.T,
+        index_query,
         index_keys,
         index_weights.T,
         query_limit.reshape(1, -1),
     )
-    return jnp.transpose(oq, (1, 0, 2)), ow[:, :JL], ok
+    return pl.pallas_call(
+        finish,
+        out_shape=(
+            jax.ShapeDtypeStruct((16, JL, DI), F32),
+            jax.ShapeDtypeStruct((16, JL), F32),
+            jax.ShapeDtypeStruct((S, DI), F32),
+        ),
+        in_specs=[vm] * 3,
+        out_specs=(vm, vm, vm),
+    )(oq, ow, ok)
 
 
 def solution(mesh):

time: 116 us -> 98.6 us (0.85)
  local copies, waits for them, and re-layouts: 10.2 us -> 0 us
  Pallas kernels: 105 us -> 97.7 us
    unnamed x5 -> x0, local copies, waits for them, and re-layouts: 10.2 us -> none
    pallas_call x1, Pallas kernels: 105 us -> 95.9 us  [per_device(): pl.pallas_call(kernel, out_shape=(jax.ShapeDtypeStruct((JL, 16, DI), F32)...]
    pallas_call x0 -> x1, Pallas kernels: none -> 1.82 us  [per_device(): pl.pallas_call(finish, out_shape=(jax.ShapeDtypeStruct((16, JL, DI), F32)...]
where the time goes in v2:
time: 98.6 us; the launch traced here: 98.4 us
  Pallas kernels  97.7 us (99%)
    pallas_call x1, Pallas kernels, per_device(): pl.pallas_call(kernel, out_shape=(jax.ShapeDtypeStruct((JL, 16, DI), F32)...  95.9 us

profile of v2, /device:TPU:24, one launch (start us, length us, event | category | flops | bytes accessed | tf_op | source)
XLA Modules:
  0.0 98.4 jit_solution(10637754425166197416)
XLA Ops:
  0.6 95.9 %shard_map.85 = (f32[16,16,128]{2,1,0:T(8,128)}, f32[16,128]{1,0:T(8,128)}, f32[512,128]{1,0:T(8,128)}) custom-call(bf16[32,576,512]{2,1,0:T(8,128)(2,1)} %bitcast.4, bf16[576,512]{1,0:T(8,128)(2,1)} %bitcast.5, bf16[512,16,128]{2,1,0:T(8,128)(2,1)} %iq_hbm.1, bf16[512,128]{1,0:T(8,128)(2,1)} %ik_hbm.1, f32[16,512]{1,0:T(8,128)} %bitcast.6, s32[1,512]{1,0:T(1,128)} %bitcast.7), custom_call_target="tpu_custom_call" | custom-call | tf_op jit(solution)/shard_map/pallas_call | solution.py:425
  96.6 1.8 %shard_map.86 = (f32[16,16,128]{2,1,0:T(8,128)}, f32[16,16]{1,0:T(8,128)}, f32[512,128]{1,0:T(8,128)}) custom-call(f32[16,16,128]{2,1,0:T(8,128)} %get-tuple-element.6.oq_ref, f32[16,128]{1,0:T(8,128)} %get-tuple-element.7.ow_ref, f32[512,128]{1,0:T(8,128)} %get-tuple-element.8.ok_ref), custom_call_target="tpu_custom_call" | custom-call | tf_op jit(solution)/shard_map/pallas_call | solution.py:493

commit v3 on v2

v3 whole, which is shorter than its diff:
```python
import functools

import jax
import jax.numpy as jnp
from jax import lax
from jax.experimental import pallas as pl
from jax.experimental.pallas import tpu as pltpu
from jax.sharding import PartitionSpec as P

H = 128
DL = 576
HI = 64
DI = 128
NK = 32
NX = 4
NY = 4
NZ = 4
C = 4
T = 128
S = 512
SQ = S // NX
U = 2 * C
JU = 8
HL = H // NX
JL = HI // NX
LOG2E = 1.4426950408889634
K2 = 2.0 * DL ** (-0.5) * LOG2E
IS = DI ** (-0.5)
HS = HI ** (-0.5)
NEG = -1e30
BIG = 3e38
MESH = pl.DeviceIdType.MESH
F32 = jnp.float32
BF16 = jnp.bfloat16


def twice(a):
    return jnp.concatenate([a, a], axis=1)


def kernel(
    q_hbm, kt_hbm, iq_hbm, ik_hbm, w_ref, lim_ref,
    oq_ref, ow_ref, ok_ref,
    qb, p_ref, s_ref, m_ref, cap_ref, ikt_ref, wj_ref,
    kt_ref, k_ref, iqr_ref, tmp_ref, iq_ref, ik_ref, ga_ref, gb_ref,
    lo_ref, l3_ref, lq_ref, ls_ref, xr_ref, lk_ref, kr_ref, lf_ref,
    st_ref, sz_ref, sa_ref, sy_ref, sb_ref, sp_ref, cc_ref,
    tg_ref, t3_ref, lg_ref, gw_ref, ka_ref,
    qp_ref, pr_ref, qs_ref, z3_ref, ys_ref, y3_ref, k3_ref, ko_ref,
    qsem, isem,
    xs_s, xs_r, kk_s, kk_r, sz_s, sz_r, sy_s, sy_r, sp_s, sp_r,
    l_s, l_r, t_s, t_r, a_s, a_r, k_s, k_r, b_s, b_r,
    pp_s, pp_r, z_s, z_r, y_s, y_r,
):
    k = lax.axis_index("keys")
    x = lax.axis_index("heads")
    core = lax.rem(k, 2)
    z = lax.rem(k // 2, NZ)
    y = k // (2 * NZ)
    sibling = k + 1 - 2 * core

    def rows_at(o):
        return pl.multiple_of(o * SQ, SQ)

    def zkey(r):
        return (y * NZ + lax.rem(z + r, NZ)) * 2 + core

    def ykey(r):
        return (lax.rem(y + r, NY) * NZ + z) * 2 + core

    myq = rows_at(x)

    def q_copy(c):
        return pltpu.make_async_copy(
            q_hbm.at[:, :, pl.ds(c * T, T)], qb.at[c % 2], qsem.at[c % 2]
        )

    def send(src, dst, ssem, rsem, kd, xd):
        pltpu.make_async_remote_copy(
            src_ref=src, dst_ref=dst, send_sem=ssem, recv_sem=rsem,
            device_id=(kd, xd), device_id_type=MESH,
        ).start()

    def wait(ref, sem):
        pltpu.make_async_copy(ref, ref, sem).wait()

    def to_keys(fn):
        def body(r, carry):
            fn(r, lax.rem(k + r, NK))
            return carry

        lax.fori_loop(1, NK, body, 0)

    def to_heads(fn):
        for r in range(1, NX):
            fn(r, lax.rem(x + r, NX))

    def reduce_send(own, three, ssem, rsem):
        to_heads(lambda r, o: send(own.at[pl.ds(rows_at(o), SQ)], three.at[r - 1], ssem, rsem, k, o))

    def reduce_sum(own, three, rsem):
        wait(three, rsem)
        return own[pl.ds(myq, SQ), :] + three[0] + three[1] + three[2]

    def gather_send(own, ssem, rsem):
        mine = own.at[pl.ds(myq, SQ)]
        to_heads(lambda r, o: send(mine, mine, ssem, rsem, k, o))

    loads = [
        pltpu.make_async_copy(a, b, isem.at[n])
        for n, (a, b) in enumerate(((iq_hbm, iqr_ref), (ik_hbm, ik_ref), (kt_hbm, kt_ref)))
    ]
    for load in loads:
        load.start()
    q_copy(0).start()
    barrier = pltpu.get_barrier_semaphore()
    to_keys(lambda r, o: pl.semaphore_signal(barrier, inc=1, device_id=(o, x), device_id_type=MESH))
    to_heads(lambda r, o: pl.semaphore_signal(barrier, inc=1, device_id=(k, o), device_id_type=MESH))

    pos = k * S + lax.broadcasted_iota(jnp.int32, (S, T), 0)
    for c in range(C):
        cap_ref[c] = jnp.where(pos <= lim_ref[0:1, c * T : (c + 1) * T], BIG, NEG)
    def prepare():
        for j in range(JL):
            wj_ref[j] = w_ref[j : j + 1, :]
        loads[1].wait()
        ikt_ref[...] = ik_ref[...].astype(F32).T.astype(BF16)
        loads[0].wait()
        for c in range(C):
            tmp_ref[...] = iqr_ref[c * T : (c + 1) * T].astype(F32).reshape(T * JL, DI)
            for j in range(JL):
                iq_ref[j, c * T : (c + 1) * T] = tmp_ref[pl.ds(j, T, stride=JL), :].astype(BF16)

    def prepare_keys():
        loads[2].wait()
        for b in range(S // 128):
            k_ref[b * 128 : (b + 1) * 128, :] = (
                kt_ref[:, b * 128 : (b + 1) * 128].astype(F32).T.astype(BF16)
            )

    def rows_of(c, jj):
        return jnp.concatenate(
            [wj_ref[2 * jj, :, c * T : (c + 1) * T], wj_ref[2 * jj + 1, :, c * T : (c + 1) * T]],
            axis=1,
        )

    def index_dots(c, jj, u):
        pair = iq_ref[pl.ds(2 * jj, 2), c * T : (c + 1) * T, :].reshape(2 * T, DI)
        s_ref[u] = lax.dot_general(
            ik_ref[...], pair, (((1,), (1,)), ((), ())), preferred_element_type=F32
        )

    def index_forward(c):
        lo_ref[c] = jnp.zeros((S, T), F32)

        def add(jj, u):
            total = None
            for v in range(2):
                row = rows_of(c, jj + v) * (IS * HS)
                term = jnp.maximum(s_ref[u + v], 0.0) * row
                part = term[:, :T] + term[:, T:]
                total = part if total is None else total + part
            lo_ref[c] += total

        def two(jj, u):
            index_dots(c, jj, u)
            index_dots(c, jj + 1, u + 1)

        two(0, 0)

        def body(i, carry):
            two(4 * i + 2, 2)
            add(4 * i, 0)
            two(jnp.minimum(4 * i + 4, JL // 2 - 2), 0)
            add(4 * i + 2, 2)
            return carry

        lax.fori_loop(0, JL // 8, body, 0)

    def logits_send(c):
        reduce_send(lo_ref.at[c], l3_ref.at[c], l_s.at[c], l_r.at[c])

    def scores(c, between):
        q_copy(c).wait()
        if c + 1 < C:
            q_copy(c + 1).start()
        slot = c % 2
        ps = c % 3

        def dots(i, u):
            h = 2 * i
            qt = jnp.concatenate([qb[slot, h], qb[slot, h + 1]], axis=1)
            s = jnp.dot(k_ref[...], qt, preferred_element_type=F32)
            s = jnp.minimum(s, twice(cap_ref[c]))
            s_ref[u] = s
            m = jnp.max(s, axis=0, keepdims=True)
            m_ref[u] = m
            st_ref[c, h, 0:1, :] = m[:, :T]
            st_ref[c, h + 1, 0:1, :] = m[:, T:]

        def soft(i, u):
            h = 2 * i
            p = jnp.exp2((s_ref[u] - m_ref[u]) * K2)
            l = jnp.sum(p, axis=0, keepdims=True)
            p_ref[ps, h] = p[:, :T]
            p_ref[ps, h + 1] = p[:, T:]
            st_ref[c, h, 1:2, :] = l[:, :T]
            st_ref[c, h + 1, 1:2, :] = l[:, T:]

        dots(0, 0)

        def body(i, carry):
            dots(2 * i + 1, 1)
            soft(2 * i, 0)
            dots(jnp.minimum(2 * i + 2, HL // 2 - 1), 0)
            soft(2 * i + 1, 1)
            return carry

        piece = HL // 4 // len(between)
        for n, action in enumerate(between):
            lax.fori_loop(n * piece, (n + 1) * piece, body, 0)
            action()
        for r in range(1, NZ):
            send(st_ref.at[c], sz_ref.at[c, r - 1], sz_s.at[c], sz_r.at[c], zkey(r), x)

    def merge(parts):
        ms = [p[:, 0, :] for p in parts]
        m = functools.reduce(jnp.maximum, ms)
        return m, sum(p[:, 1, :] * jnp.exp2((a - m) * K2) for a, p in zip(ms, parts))

    def stats_y(c):
        wait(sz_ref.at[c], sz_r.at[c])
        m, total = merge([st_ref[c]] + [sz_ref[c, r] for r in range(NZ - 1)])
        sa_ref[c, :, 0, :] = m
        sa_ref[c, :, 1, :] = total
        for r in range(1, NY):
            send(sa_ref.at[c], sy_ref.at[c, r - 1], sy_s.at[c], sy_r.at[c], ykey(r), x)

    def stats_core(c):
        wait(sy_ref.at[c], sy_r.at[c])
        m, total = merge([sa_ref[c]] + [sy_ref[c, r] for r in range(NY - 1)])
        sb_ref[c, :, 0, :] = m
        sb_ref[c, :, 1, :] = total
        send(sb_ref.at[c], sp_ref.at[c], sp_s.at[c], sp_r.at[c], sibling, x)

    def logit_stats():
        for c in range(C):
            v = reduce_sum(lo_ref.at[c], l3_ref.at[c], l_r.at[c])
            v = jnp.minimum(v, cap_ref[c, pl.ds(myq, SQ), :])
            lq_ref[c] = v
            m = jnp.max(v, axis=0, keepdims=True)
            ls_ref[c, 0:1, :] = m
            ls_ref[c, 1:2, :] = jnp.sum(jnp.exp(v - m), axis=0, keepdims=True)
        to_heads(lambda r, o: send(ls_ref, xr_ref.at[r - 1], xs_s, xs_r, k, o))

    def logit_stats_heads():
        wait(xr_ref, xs_r)
        for c in range(C):
            ms = [ls_ref[c, 0:1, :]] + [xr_ref[r, c, 0:1, :] for r in range(NX - 1)]
            ts = [ls_ref[c, 1:2, :]] + [xr_ref[r, c, 1:2, :] for r in range(NX - 1)]
            m = functools.reduce(jnp.maximum, ms)
            lk_ref[c, 0:1, :] = m
            lk_ref[c, 1:2, :] = sum(t * jnp.exp(a - m) for a, t in zip(ms, ts))
        to_keys(lambda r, o: send(lk_ref, kr_ref.at[r - 1], kk_s, kk_r, o, x))

    def logit_stats_keys():
        wait(kr_ref, kk_r)
        for c in range(C):
            own_m, own_t = lk_ref[c, 0:1, :], lk_ref[c, 1:2, :]
            ms = kr_ref[:, c, 0, :]
            ts = kr_ref[:, c, 1, :]
            m = jnp.maximum(own_m, jnp.max(ms, axis=0, keepdims=True))
            lf_ref[c, 0:1, :] = m
            lf_ref[c, 1:2, :] = own_t * jnp.exp(own_m - m) + jnp.sum(
                ts * jnp.exp(ms - m), axis=0, keepdims=True
            )

    def target(c):
        wait(sp_ref.at[c], sp_r.at[c])
        m, total = merge([sb_ref[c], sp_ref[c]])
        cc_ref[...] = jnp.exp2((st_ref[c, :, 0, :] - m) * K2) / (total * H)
        ps = c % 3
        rows = 64

        def body(b, carry):
            at = pl.ds(pl.multiple_of(b * rows, rows), rows)
            acc = p_ref[ps, 0, at, :] * cc_ref[0:1, :]
            for h in range(1, HL):
                acc += p_ref[ps, h, at, :] * cc_ref[h : h + 1, :]
            tg_ref[c, at, :] = acc
            return carry

        lax.fori_loop(0, S // rows, body, 0)
        reduce_send(tg_ref.at[c], t3_ref.at[c], t_s.at[c], t_r.at[c])

    def logit_grad(c):
        t = reduce_sum(tg_ref.at[c], t3_ref.at[c], t_r.at[c])
        v = lq_ref[c]
        probs = jnp.where(
            cap_ref[c, pl.ds(myq, SQ), :] > 0, jnp.exp(v - lf_ref[c, 0:1, :]), 0.0
        ) / lf_ref[c, 1:2, :]
        span = (lim_ref[0:1, c * T : (c + 1) * T] + 1).astype(F32)
        lg_ref[c, pl.ds(myq, SQ), :] = (probs - t) * span
        gather_send(lg_ref.at[c], a_s.at[c], a_r.at[c])

    def grads(c, half):
        unit = 2 * c + half
        base = JU * half
        if half == 0:
            wait(t3_ref.at[c], a_r.at[c])

        def gate(jj, u, out, at):
            dots = s_ref[u]
            lg = twice(lg_ref[c])
            gw = jnp.sum(lg * jnp.maximum(dots, 0.0), axis=0, keepdims=True) * (IS * HS)
            at_j = 2 * jj - base
            gw_ref[at_j : at_j + 1, :] = gw[:, :T]
            gw_ref[at_j + 1 : at_j + 2, :] = gw[:, T:]
            g = jnp.where(dots > 0, lg * (rows_of(c, jj) * HS), 0.0)
            out[:, at : at + 2 * T] = g.astype(BF16)

        def products(g_ref, j0):
            g = g_ref[...]
            four = iq_ref[j0 : j0 + 4, c * T : (c + 1) * T, :].reshape(4 * T, DI)
            qpt = jnp.dot(ikt_ref[...], g, preferred_element_type=F32) * IS
            for u in range(4):
                qp = qpt[:, u * T : (u + 1) * T].T
                for zz in range(NZ):
                    for cr in range(2):
                        at = (zz * 2 + cr) * 16
                        qp_ref[unit, cr, zz, j0 - base + u] = qp[at : at + 16]
            ka_ref[...] += jnp.dot(g, four, preferred_element_type=F32)

        first = base // 2
        index_dots(c, first, 0)
        for u in range(4):
            if u < 3:
                index_dots(c, first + u + 1, (u + 1) % 2)
            gate(first + u, u % 2, ga_ref if u < 2 else gb_ref, (u % 2) * 2 * T)
            if u == 1:
                products(ga_ref, base)
        products(gb_ref, base + 4)
        gwt = gw_ref[...].T
        for zz in range(NZ):
            for cr in range(2):
                at = (zz * 2 + cr) * 16
                qp_ref[unit, cr, zz, JU] = gwt[at : at + 16]
        send(
            qp_ref.at[unit, 1 - core], pr_ref.at[unit], pp_s.at[unit], pp_r.at[unit], sibling, x
        )

    def pair_sum(u):
        wait(pr_ref.at[u], pp_r.at[u])
        for zz in range(NZ):
            qs_ref[u, zz] = qp_ref[u, core, zz] + pr_ref[u, zz]
        for r in range(1, NZ):
            send(
                qs_ref.at[u, lax.rem(z + r, NZ)], z3_ref.at[u, r - 1], z_s.at[u], z_r.at[u], zkey(r), x
            )

    def plane_sum(u):
        wait(z3_ref.at[u], z_r.at[u])
        ys_ref[u] = qs_ref[u, z] + z3_ref[u, 0] + z3_ref[u, 1] + z3_ref[u, 2]
        away = lax.rem(y - u // 2 + NY, NY)

        @pl.when(away != 0)
        def _():
            send(ys_ref.at[u], y3_ref.at[u % 2, away - 1], y_s.at[u], y_r.at[u % 2], ykey(NY - away), x)

    def key_send():
        reduce_send(ka_ref, k3_ref, k_s, k_r)

    def key_sum():
        ko_ref[pl.ds(myq, SQ), :] = reduce_sum(ka_ref, k3_ref, k_r) * IS
        gather_send(ko_ref, b_s, b_r)

    gw_ref[...] = jnp.zeros_like(gw_ref)
    ka_ref[...] = jnp.zeros_like(ka_ref)

    def nothing():
        pass

    def sched(*steps):
        def run():
            for step, arg in steps:
                if arg is None:
                    step()
                else:
                    step(arg)

        return run

    def each(step, *units):
        for u in units:
            step(u)

    prepare()
    index_forward(0)
    index_forward(1)
    pl.semaphore_wait(barrier, NK - 1 + NX - 1)
    logits_send(0)
    logits_send(1)
    index_forward(2)
    logits_send(2)
    index_forward(3)
    logits_send(3)
    prepare_keys()
    scores(0, (nothing,))
    scores(1, (nothing, nothing, sched((stats_y, 0)), sched((logit_stats, None))))
    scores(2, (
        sched((stats_core, 0)), sched((target, 0), (logit_stats_heads, None)), sched((stats_y, 1)), nothing,
    ))
    scores(3, (
        sched((stats_core, 1)), sched((logit_stats_keys, None), (logit_grad, 0), (target, 1)),
        sched((stats_y, 2)), nothing,
    ))
    grads(0, 0)
    stats_core(2)
    logit_grad(1)
    target(2)
    grads(0, 1)
    stats_y(3)
    each(pair_sum, 0, 1)
    stats_core(3)
    grads(1, 0)
    logit_grad(2)
    target(3)
    grads(1, 1)
    each(pair_sum, 2, 3)
    each(plane_sum, 0, 1)
    grads(2, 0)
    grads(2, 1)
    logit_grad(3)
    each(pair_sum, 4, 5)
    each(plane_sum, 2, 3)
    grads(3, 0)
    grads(3, 1)
    key_send()
    each(pair_sum, 6, 7)
    each(plane_sum, 4, 5)
    key_sum()
    each(plane_sum, 6, 7)
    for half in range(2):
        wait(y3_ref.at[half], y_r.at[half])
        three = y3_ref.at[half]
        mine = ys_ref[2 * y + half] + three[0] + three[1] + three[2]
        oq_ref[half * JU : (half + 1) * JU] = mine[:JU]
        ow_ref[half] = mine[JU]
    wait(k3_ref, b_r)
    ok_ref[...] = ko_ref[...]

    wait(xr_ref, xs_s)
    wait(kr_ref, kk_s)
    wait(k3_ref, k_s)
    wait(k3_ref, b_s)
    for c in range(C):
        wait(l3_ref.at[c], l_s.at[c])
        wait(t3_ref.at[c], t_s.at[c])
        wait(t3_ref.at[c], a_s.at[c])
        wait(sz_ref.at[c], sz_s.at[c])
        wait(sy_ref.at[c], sy_s.at[c])
        wait(sp_ref.at[c], sp_s.at[c])
    for u in range(U):
        wait(pr_ref.at[u], pp_s.at[u])
        wait(z3_ref.at[u], z_s.at[u])

        @pl.when(y != u // 2)
        def _():
            wait(ys_ref.at[u], y_s.at[u])


def finish(oq_ref, ow_ref, ok_ref, q_ref, w_ref, k_ref):
    for j in range(JL):
        q_ref[:, j, :] = oq_ref[j]
    for half in range(2):
        w_ref[:, half * JU : (half + 1) * JU] = ow_ref[half, :, :JU]
    k_ref[...] = ok_ref[...]


def per_device(main_query, latent_keys, index_query, index_keys, index_weights, query_limit):
    vm = pl.BlockSpec(memory_space=pltpu.VMEM)
    dma = pltpu.SemaphoreType.DMA
    oq, ow, ok = pl.pallas_call(
        kernel,
        out_shape=(
            jax.ShapeDtypeStruct((JL, 16, DI), F32),
            jax.ShapeDtypeStruct((2, 16, DI), F32),
            jax.ShapeDtypeStruct((S, DI), F32),
        ),
        in_specs=[pl.BlockSpec(memory_space=pl.ANY)] * 4 + [vm] * 2,
        out_specs=(vm, vm, vm),
        scratch_shapes=[
            pltpu.VMEM((2, HL, DL, T), BF16),
            pltpu.VMEM((3, HL, S, T), F32),
            pltpu.VMEM((4, S, 2 * T), F32),
            pltpu.VMEM((2, 1, 2 * T), F32),
            pltpu.VMEM((C, S, T), F32),
            pltpu.VMEM((DI, S), BF16),
            pltpu.VMEM((JL, 1, C * T), F32),
            pltpu.VMEM((DL, S), BF16),
            pltpu.VMEM((S, DL), BF16),
            pltpu.VMEM((C * T, JL, DI), BF16),
            pltpu.VMEM((T * JL, DI), F32),
            pltpu.VMEM((JL, C * T, DI), BF16),
            pltpu.VMEM((S, DI), BF16),
            pltpu.VMEM((S, 4 * T), BF16),
            pltpu.VMEM((S, 4 * T), BF16),
            pltpu.VMEM((C, S, T), F32),
            pltpu.VMEM((C, NX - 1, SQ, T), F32),
            pltpu.VMEM((C, SQ, T), F32),
            pltpu.VMEM((C, 2, T), F32),
            pltpu.VMEM((NX - 1, C, 2, T), F32),
            pltpu.VMEM((C, 2, T), F32),
            pltpu.VMEM((NK - 1, C, 2, T), F32),
            pltpu.VMEM((C, 2, T), F32),
            pltpu.VMEM((C, HL, 2, T), F32),
            pltpu.VMEM((C, NZ - 1, HL, 2, T), F32),
            pltpu.VMEM((C, HL, 2, T), F32),
            pltpu.VMEM((C, NY - 1, HL, 2, T), F32),
            pltpu.VMEM((C, HL, 2, T), F32),
            pltpu.VMEM((C, HL, 2, T), F32),
            pltpu.VMEM((HL, T), F32),
            pltpu.VMEM((C, S, T), F32),
            pltpu.VMEM((C, NX - 1, SQ, T), F32),
            pltpu.VMEM((C, S, T), F32),
            pltpu.VMEM((DI, T), F32),
            pltpu.VMEM((S, DI), F32),
            pltpu.VMEM((U, 2, NZ, JU + 1, 16, DI), F32),
            pltpu.VMEM((U, NZ, JU + 1, 16, DI), F32),
            pltpu.VMEM((U, NZ, JU + 1, 16, DI), F32),
            pltpu.VMEM((U, NZ - 1, JU + 1, 16, DI), F32),
            pltpu.VMEM((U, JU + 1, 16, DI), F32),
            pltpu.VMEM((2, NY - 1, JU + 1, 16, DI), F32),
            pltpu.VMEM((NX - 1, SQ, DI), F32),
            pltpu.VMEM((S, DI), F32),
            dma((2,)), dma((3,)),
            dma, dma, dma, dma,
            *[dma((C,))] * 12, dma, dma, dma, dma,
            *[dma((U,))] * 5, dma((2,)),
        ],
        compiler_params=pltpu.CompilerParams(
            collective_id=0, has_side_effects=True, vmem_limit_bytes=67043328
        ),
    )(
        jnp.transpose(main_query, (1, 2, 0)),
        latent_keys.T,
        index_query,
        index_keys,
        index_weights.T,
        query_limit.reshape(1, -1),
    )
    return pl.pallas_call(
        finish,
        out_shape=(
            jax.ShapeDtypeStruct((16, JL, DI), F32),
            jax.ShapeDtypeStruct((16, JL), F32),
            jax.ShapeDtypeStruct((S, DI), F32),
        ),
        in_specs=[vm] * 3,
        out_specs=(vm, vm, vm),
    )(oq, ow, ok)


def solution(mesh):
    in_specs = (
        P(None, "heads", None),
        P("keys", None),
        P(None, "heads", None),
        P("keys", None),
        P(None, "heads"),
        P(),
    )
    out_specs = (P("keys", "heads", None), P("keys", "heads"), P("keys", None))
    return jax.shard_map(
        per_device, mesh=mesh, in_specs=in_specs, out_specs=out_specs, check_vma=False
    )
```

time: 98.6 us -> 88.4 us (0.90)
  Pallas kernels: 97.7 us -> 87.4 us
    pallas_call x1, Pallas kernels: 95.9 us -> 85.5 us  [per_device(): pl.pallas_call(kernel, out_shape=(jax.ShapeDtypeStruct((JL, 16, DI), F32)...]
where the time goes in v3:
time: 88.4 us; the launch traced here: 88 us
  Pallas kernels  87.4 us (99%)
    pallas_call x1, Pallas kernels, per_device(): pl.pallas_call(kernel, out_shape=(jax.ShapeDtypeStruct((JL, 16, DI), F32)...  85.5 us
    pallas_call x1, Pallas kernels, per_device(): pl.pallas_call(finish, out_shape=(jax.ShapeDtypeStruct((16, JL, DI), F32)...  1.88 us

profile of v3, /device:TPU:24, one launch (start us, length us, event | category | flops | bytes accessed | tf_op | source)
XLA Modules:
  0.0 88.0 jit_solution(1233369164928243533)
XLA Ops:
  0.6 85.5 %shard_map.85 = (f32[16,16,128]{2,1,0:T(8,128)}, f32[2,16,128]{2,1,0:T(8,128)}, f32[512,128]{1,0:T(8,128)}) custom-call(bf16[32,576,512]{2,1,0:T(8,128)(2,1)} %bitcast.4, bf16[576,512]{1,0:T(8,128)(2,1)} %bitcast.5, bf16[512,16,128]{2,1,0:T(8,128)(2,1)} %iq_hbm.1, bf16[512,128]{1,0:T(8,128)(2,1)} %ik_hbm.1, f32[16,512]{1,0:T(8,128)} %bitcast.6, s32[1,512]{1,0:T(1,128)} %bitcast.7), custom_call_target="tpu_custom_call" | custom-call | tf_op jit(solution)/shard_map/pallas_call | solution.py:483
  86.1 1.9 %shard_map.86 = (f32[16,16,128]{2,1,0:T(8,128)}, f32[16,16]{1,0:T(8,128)}, f32[512,128]{1,0:T(8,128)}) custom-call(f32[16,16,128]{2,1,0:T(8,128)} %get-tuple-element.6.oq_ref, f32[2,16,128]{2,1,0:T(8,128)} %get-tuple-element.7.ow_ref, f32[512,128]{1,0:T(8,128)} %get-tuple-element.8.ok_ref), custom_call_target="tpu_custom_call" | custom-call | tf_op jit(solution)/shard_map/pallas_call | solution.py:552

commit v4 on v3

--- a/solution.py
+++ b/solution.py
@@ -408,29 +408,30 @@
     scores(0, (nothing,))
     scores(1, (nothing, nothing, sched((stats_y, 0)), sched((logit_stats, None))))
     scores(2, (
-        sched((stats_core, 0)), sched((target, 0), (logit_stats_heads, None)), sched((stats_y, 1)), nothing,
+        nothing, sched((stats_core, 0), (logit_stats_heads, None)), sched((target, 0), (stats_y, 1)), nothing,
     ))
     scores(3, (
-        sched((stats_core, 1)), sched((logit_stats_keys, None), (logit_grad, 0), (target, 1)),
-        sched((stats_y, 2)), nothing,
+        sched((stats_core, 1)), sched((logit_stats_keys, None), (logit_grad, 0)),
+        sched((stats_y, 2), (target, 1)), nothing,
     ))
+    stats_core(2)
     grads(0, 0)
-    stats_core(2)
+    stats_y(3)
+    target(2)
     logit_grad(1)
-    target(2)
     grads(0, 1)
-    stats_y(3)
-    each(pair_sum, 0, 1)
+    pair_sum(0)
     stats_core(3)
+    pair_sum(1)
+    target(3)
+    logit_grad(2)
     grads(1, 0)
-    logit_grad(2)
-    target(3)
     grads(1, 1)
+    each(plane_sum, 0, 1)
     each(pair_sum, 2, 3)
-    each(plane_sum, 0, 1)
+    logit_grad(3)
     grads(2, 0)
     grads(2, 1)
-    logit_grad(3)
     each(pair_sum, 4, 5)
     each(plane_sum, 2, 3)
     grads(3, 0)

time: 88.4 us -> 86.8 us (0.982)
  Pallas kernels: 87.4 us -> 85.9 us
    pallas_call x1, Pallas kernels: 85.5 us -> 84.1 us  [per_device(): pl.pallas_call(kernel, out_shape=(jax.ShapeDtypeStruct((JL, 16, DI), F32)...]
where the time goes in v4:
time: 86.8 us; the launch traced here: 86.6 us
  Pallas kernels  85.9 us (99%)
    pallas_call x1, Pallas kernels, per_device(): pl.pallas_call(kernel, out_shape=(jax.ShapeDtypeStruct((JL, 16, DI), F32)...  84.1 us
    pallas_call x1, Pallas kernels, per_device(): pl.pallas_call(finish, out_shape=(jax.ShapeDtypeStruct((16, JL, DI), F32)...  1.88 us

profile of v4, /device:TPU:24, one launch (start us, length us, event | category | flops | bytes accessed | tf_op | source)
XLA Modules:
  0.0 86.6 jit_solution(16675226246501081918)
XLA Ops:
  0.6 84.1 %shard_map.85 = (f32[16,16,128]{2,1,0:T(8,128)}, f32[2,16,128]{2,1,0:T(8,128)}, f32[512,128]{1,0:T(8,128)}) custom-call(bf16[32,576,512]{2,1,0:T(8,128)(2,1)} %bitcast.4, bf16[576,512]{1,0:T(8,128)(2,1)} %bitcast.5, bf16[512,16,128]{2,1,0:T(8,128)(2,1)} %iq_hbm.1, bf16[512,128]{1,0:T(8,128)(2,1)} %ik_hbm.1, f32[16,512]{1,0:T(8,128)} %bitcast.6, s32[1,512]{1,0:T(1,128)} %bitcast.7), custom_call_target="tpu_custom_call" | custom-call | tf_op jit(solution)/shard_map/pallas_call | solution.py:484
  84.7 1.9 %shard_map.86 = (f32[16,16,128]{2,1,0:T(8,128)}, f32[16,16]{1,0:T(8,128)}, f32[512,128]{1,0:T(8,128)}) custom-call(f32[16,16,128]{2,1,0:T(8,128)} %get-tuple-element.6.oq_ref, f32[2,16,128]{2,1,0:T(8,128)} %get-tuple-element.7.ow_ref, f32[512,128]{1,0:T(8,128)} %get-tuple-element.8.ok_ref), custom_call_target="tpu_custom_call" | custom-call | tf_op jit(solution)/shard_map/pallas_call | solution.py:553
